TPU v7x, 32 devices: a whole 2x2x4 slice. The times are simulated.
32 devices in a mesh: rows: 8 (over z, x), scales: 4 (over y, core).
Axes of the slice: x: 2, y: 2, z: 4, core: 2. Of those that a mesh axis runs over, the one named last changes fastest.
Arguments:
- image_now: float32 [256, 8192], P(('rows', 'scales')), may hold values from 0.1 to 4
- gradient: float32 [256, 8192], P(('rows', 'scales')), may hold values from -140 to 140
- hessian_weight: float32 [256, 8192], P(('rows', 'scales')), may hold values from 0.1 to 10
- psf_tiles: float32 [32, 256], P(('rows', 'scales')), may hold values from -0.5 to 1.7
- facet_of_row: int32 [256], P(('rows', 'scales')), may hold values from 0 to 31, never falling along the last dimension, each value on 1 to 32 neighbouring positions
- tile_slot: int32 [32], replicated, may hold values from 0 to 31, each once
- thresholds: float32 [4], replicated, may hold values from 0.2 to 2
Outputs:
- new_image: float32 [256, 8192], P(('rows', 'scales'))
Inputs may be any that keep to these rules, and one draw needn't show every extreme that they name: `facet_of_row`: facet numbers never fall along the rows; every facet covers 1 to 32 rows, and some facet exactly 32. `tile_slot`: each facet's tile stands in a different row of psf_tiles, and every row holds one.
All inputs are finite; a program needn't handle non-finite values.
Results may differ from a plain program's by a relative error of at most 0.0001.
Values sent between devices are 32-bit elements; how exact they have to be, the bound alone decides.
A program may use at most 64 MiB of HBM per device.

v0:
```python
import jax
import jax.numpy as jnp
from jax import lax
from jax.sharding import PartitionSpec as P

TILE = 16
SUBITERS = 2
SPLINE_EDGE = 0.0625
SPLINE_NEAR = 0.25
SPLINE_MID = 0.375


def padded_2(cells, sides, width):
    for axis, dim in sides:
        count = lax.axis_size(axis)
        ends = count - 1
        head = lax.slice_in_dim(cells, 0, width, axis=dim)
        tail = lax.slice_in_dim(cells, cells.shape[dim] - width, cells.shape[dim], axis=dim)
        cells = jnp.concatenate(
            [
                lax.ppermute(tail, axis, [(i, (i + 1) % count) for i in range(ends)]),
                cells,
                lax.ppermute(head, axis, [((i + 1) % count, i) for i in range(ends)]),
            ],
            axis=dim,
        )
    return cells


def along_columns(source, spacing):
    length = source.shape[1]
    padded = jnp.pad(source, ((0, 0), (2 * spacing, 2 * spacing)))
    outer_pair = padded[:, 0:length] + padded[:, 4 * spacing : 4 * spacing + length]
    inner_pair = (
        padded[:, spacing : spacing + length] + padded[:, 3 * spacing : 3 * spacing + length]
    )
    return SPLINE_EDGE * outer_pair + SPLINE_NEAR * inner_pair + SPLINE_MID * source


def rows_traced(source, spacing, reach):
    length = source.shape[0]
    padded = jnp.pad(source, ((reach, reach), (0, 0)))

    def shifted_rows(offset):
        return lax.dynamic_slice_in_dim(padded, reach + offset, length, 0)

    outer_pair = shifted_rows(-2 * spacing) + shifted_rows(2 * spacing)
    inner_pair = shifted_rows(-spacing) + shifted_rows(spacing)
    return SPLINE_EDGE * outer_pair + SPLINE_NEAR * inner_pair + SPLINE_MID * source


def widen_band(source):
    half_tile = TILE // 2
    extended = padded_2(source, ((("rows", "scales"), 0),), half_tile)
    return jnp.pad(extended, ((0, 0), (half_tile, half_tile)))


def forward_blur(source, weights):
    band_rows, columns = source.shape
    padded = widen_band(source)

    def forward_add_tap_row(tap_row, summed):
        shifted = lax.dynamic_slice_in_dim(padded, tap_row, band_rows, 0)
        tap_weights = lax.dynamic_index_in_dim(weights, tap_row, 1, keepdims=False)
        for column in range(TILE):
            summed = (
                summed + tap_weights[:, column : column + 1] * shifted[:, column : column + columns]
            )
        return summed

    return lax.fori_loop(0, TILE, forward_add_tap_row, jnp.zeros((band_rows, columns), jnp.float32))


def adjoint_blur(source, wide_weights):
    band_rows, columns = source.shape
    half_tile = TILE // 2
    padded = widen_band(source)

    def adjoint_add_tap_row(tap_row, summed):
        offset = 2 * half_tile - tap_row
        shifted = lax.dynamic_slice_in_dim(padded, offset, band_rows, 0)
        weight_rows = lax.dynamic_slice_in_dim(wide_weights, offset, band_rows, 0)
        tap_weights = lax.dynamic_index_in_dim(weight_rows, tap_row, 1, keepdims=False)
        for column in range(TILE):
            offset_col = 2 * half_tile - column
            summed = (
                summed
                + tap_weights[:, column : column + 1]
                * shifted[:, offset_col : offset_col + columns]
            )
        return summed

    return lax.fori_loop(0, TILE, adjoint_add_tap_row, jnp.zeros((band_rows, columns), jnp.float32))


def body(image_now, gradient, hessian_weight, psf_tiles, facet_of_row, tile_slot, thresholds):
    band_rows, columns = image_now.shape
    half_tile = TILE // 2
    scale_count = lax.axis_size("scales")
    scale_index = lax.axis_index("scales")
    facet_ids = jnp.arange(tile_slot.shape[0], dtype=jnp.int32)
    slot_rows = jnp.sum(
        jnp.where(facet_of_row[:, None] == facet_ids[None, :], tile_slot[None, :], 0), axis=1
    )
    tiles_in = lax.all_gather(psf_tiles, ("rows", "scales"), axis=0, tiled=True)
    length = tiles_in.shape[0]
    onehot = (slot_rows[:, None] == jnp.arange(length, dtype=jnp.int32)[None, :]).astype(
        jnp.float32
    )
    flat_rows = jnp.dot(
        onehot, tiles_in, precision=lax.Precision.HIGHEST, preferred_element_type=jnp.float32
    )
    wide_rows = padded_2(flat_rows, ((("rows", "scales"), 0),), half_tile)
    weights = flat_rows.reshape(band_rows, TILE, TILE)
    wide_weights = wide_rows.reshape(band_rows + 2 * half_tile, TILE, TILE)
    level_gain = jnp.sum(jnp.where(jnp.arange(scale_count) == scale_index, thresholds, 0.0))
    reach = 2**scale_count

    def column_level(depth, plane):
        return rows_traced(plane, jnp.left_shift(jnp.int32(1), depth), reach)

    current = image_now
    for sweep in range(SUBITERS):
        change = current - image_now
        pushed = hessian_weight * forward_blur(change, weights)
        descent = gradient + adjoint_blur(pushed, wide_weights)
        blurred = forward_blur(descent, weights)
        totals = lax.psum(
            (jnp.sum(descent * descent), jnp.sum(hessian_weight * blurred * blurred)),
            ("rows", "scales"),
        )
        step_size = totals[0] / totals[1]
        trial = current - step_size * descent
        stripe = lax.all_gather(trial, "scales", axis=0, tiled=True)
        smooth = stripe
        lower = jnp.zeros_like(stripe)
        upper = jnp.zeros_like(stripe)
        for depth in range(scale_count):
            smoother = along_columns(smooth, 2**depth)
            lower = jnp.where(scale_index == depth, smooth, lower)
            upper = jnp.where(scale_index == depth, smoother, upper)
            smooth = smoother
        limit = step_size * level_gain
        lower_cols, upper_cols = (
            lax.all_to_all(lower, "rows", split_axis=1, concat_axis=0, tiled=True),
            lax.all_to_all(upper, "rows", split_axis=1, concat_axis=0, tiled=True),
        )
        lower_cols = lax.fori_loop(0, scale_index, column_level, lower_cols)
        upper_cols = lax.fori_loop(0, scale_index + 1, column_level, upper_cols)
        detail = lower_cols - upper_cols
        kept = (
            detail
            - jnp.clip(detail, -limit, limit)
            + jnp.where(scale_index == scale_count - 1, upper_cols, 0.0)
        )
        contribution = lax.all_to_all(kept, "rows", split_axis=0, concat_axis=1, tiled=True)
        current = lax.psum_scatter(contribution, "scales", scatter_dimension=0, tiled=True)
    return current


def solution(mesh):
    in_specs = (
        P(("rows", "scales"), None),
        P(("rows", "scales"), None),
        P(("rows", "scales"), None),
        P(("rows", "scales"), None),
        P(("rows", "scales")),
        P(),
        P(),
    )
    out_specs = P(("rows", "scales"), None)
    return jax.shard_map(body, mesh=mesh, in_specs=in_specs, out_specs=out_specs, check_vma=False)
```

profile of v0, /device:TPU:0, one launch (start us, length us, event | category | flops | bytes accessed | tf_op | source)
XLA Modules:
  0.0 672.7 jit_solution(16924233468898300590)
XLA Ops:
  7.6 2.4 collective-permute-start.2
  12.2 45.4 %all-gather = f32[32,1,256]{2,1,0:T(1,128)S(1)} all-gather(f32[1,1,256]{2,1,0:T(1,128)} %bitcast.79), channel_id=1, replica_groups=mesh['rows'=8,'scales'=4] {'rows','scales'}, dimensions={0}, use_global_device_ids=true | all-gather | bytes 33792 | tf_op jit(solution)/shard_map/all_gather | solution.py:105
  58.2 27.8 %while.146 = (s32[]{:T(128)}, f32[8,8192]{1,0:T(8,128)S(1)}, f32[8,16,16]{2,0,1:T(8,128)S(1)}, f32[24,8208]{1,0:T(8,128)S(1)}, s32[]{:T(128)}, /*index=5*/s32[]{...) while((s32[]{:T(128)}, f32[8,8192]{1,0:T(8,128)S(1)}, ...), condition=%wide.region_2.3_spmd.clone, body=%wide.region_1.2_spmd.clone.sunk | while | flops 2162706 | bytes 4721599 | solution.py:71
  89.7 3.0 collective-permute-start
  94.0 2.5 collective-permute-done.1
  97.0 29.6 %while.147 = (s32[]{:T(128)}, f32[8,8192]{1,0:T(8,128)S(1)}, f32[24,16,16]{2,0,1:T(8,128)S(1)}, f32[24,8208]{1,0:T(8,128)S(1)}, s32[]{:T(128)}, /*index=5*/s32[]...) while((s32[]{:T(128)}, f32[8,8192]{1,0:T(8,128)S(1)}, ...), condition=%wide.region_4.5_spmd.clone, body=%wide.region_3.4_spmd.clone.sunk | while | flops 2162713 | bytes 4721729 | solution.py:93
  127.3 4.3 collective-permute-start.6
  135.3 27.8 %while.148 = (s32[]{:T(128)}, f32[8,8192]{1,0:T(8,128)S(1)}, f32[8,16,16]{2,0,1:T(8,128)S(1)}, f32[24,8208]{1,0:T(8,128)S(1)}, s32[]{:T(128)}, /*index=5*/s32[]{...) while((s32[]{:T(128)}, f32[8,8192]{1,0:T(8,128)S(1)}, ...), condition=%wide.region_8.9_spmd.clone, body=%wide.region_7.8_spmd.clone.sunk | while | flops 2162706 | bytes 4721599 | solution.py:71
  163.9 42.4 %all-reduce.19 = (f32[]{:T(128)}, f32[]{:T(128)}) all-reduce(f32[]{:T(128)} %get-tuple-element.1221, f32[]{:T(128)} %fusion.137), channel_id=1, replica_groups=mesh['rows'=8,'scales'=4] {'rows','scales'}, use_global_device_ids=true, to_apply=%region_6.7 | all-reduce | flops 2 | bytes 16 | tf_op jit(solution)/shard_map/psum | solution.py:128
  208.5 17.4 %all-gather.4.cloned.1.call-done = f32[32,8192]{1,0:T(8,128)} async-done(((f32[8,8192]{1,0:T(8,128)}), f32[32,8192]{1,0:T(8,128)}) %all-gather.4.cloned.1.call-update) | async-done | bytes 1048592 | tf_op jit(solution)/shard_map/all_gather | solution.py:134
  225.8 4.2 multiply_add_fusion.5
  236.8 5.5 all-to-all-start.1
  243.4 25.1 %all-to-all-done.1 = f32[32,8,1024]{2,0,1:T(8,128)S(1)} async-done(((f32[32,8,1024]{2,0,1:T(8,128)}), f32[32,8,1024]{2,0,1:T(8,128)S(1)}, u32[]{:S(2)}, u32[]{:S(2)}) %all-to-all-start.1) | async-done | bytes 1048608 | tf_op jit(solution)/shard_map/all_to_all | solution.py:146
  268.5 3.8 all-to-all-start
  274.4 23.8 %all-to-all-done = f32[32,8,1024]{2,0,1:T(8,128)S(1)} async-done(((f32[32,8,1024]{2,0,1:T(8,128)}), f32[32,8,1024]{2,0,1:T(8,128)S(1)}, u32[]{:S(2)}, u32[]{:S(2)}) %all-to-all-start) | async-done | bytes 1048608 | tf_op jit(solution)/shard_map/all_to_all | solution.py:145
  298.5 30.1 %all_to_all.114 = f32[8,32,1024]{2,1,0:T(8,128)S(1)} all-to-all(f32[8,32,1024]{2,1,0:T(8,128)S(1)} %bitcast.72), channel_id=1, replica_groups=mesh['rows'=8,'scales'=4] {'rows'}, dimensions={0} | all-to-all | bytes 2097152 | tf_op jit(solution)/shard_map/all_to_all | solution.py:156
  329.9 24.7 %reduce-scatter.3.cloned.1.call-done = f32[8,8192]{1,0:T(8,128)} async-done(((f32[32,8192]{1,0:T(8,128)}), f32[8,8192]{1,0:T(8,128)}) %reduce-scatter.3.cloned.1.call-update) | async-done | bytes 262160 | tf_op jit(solution)/shard_map/reduce_scatter | solution.py:157
  358.5 2.4 collective-permute-done.9
  361.2 27.8 %while.149 = (s32[]{:T(128)}, f32[8,8192]{1,0:T(8,128)S(1)}, f32[8,16,16]{2,0,1:T(8,128)S(1)}, f32[24,8208]{1,0:T(8,128)S(1)}, s32[]{:T(128)}, /*index=5*/s32[]{...) while((s32[]{:T(128)}, f32[8,8192]{1,0:T(8,128)S(1)}, ...), condition=%wide.region_18.19_spmd.clone, body=%wide.region_17.18_spmd.clone.sunk | while | flops 2162706 | bytes 4721599 | solution.py:71
  389.0 6.7 collective-permute-start.10
  399.4 29.6 %while.150 = (s32[]{:T(128)}, f32[8,8192]{1,0:T(8,128)S(1)}, f32[24,16,16]{2,0,1:T(8,128)S(1)}, f32[24,8208]{1,0:T(8,128)S(1)}, s32[]{:T(128)}, /*index=5*/s32[]...) while((s32[]{:T(128)}, f32[8,8192]{1,0:T(8,128)S(1)}, ...), condition=%wide.region_20.21_spmd.clone, body=%wide.region_19.20_spmd.clone.sunk | while | flops 2162713 | bytes 4721729 | solution.py:93
  429.6 8.0 %collective-permute-start.12 = (f32[8,8192]{1,0:T(8,128)S(1)}, f32[8,8192]{1,0:T(8,128)S(1)}, u32[]{:S(2)}, u32[]{:S(2)}) collective-permute-start(f32[8,8192]{1,0:T(8,128)S(1)} %get-tuple-element.1218), channel_id=1, source_target_pairs={{0,1},{1,2},{2,3},{3,4},{4,5},{5,6},{6,7},{7,8},{8,9},{9,10},{10,1... | collective-permute-start | bytes 786440 | tf_op jit(solution)/shard_map/ppermute | solution.py:21
  441.4 27.8 %while.151 = (s32[]{:T(128)}, f32[8,8192]{1,0:T(8,128)S(1)}, f32[8,16,16]{2,0,1:T(8,128)S(1)}, f32[24,8208]{1,0:T(8,128)S(1)}, s32[]{:T(128)}, /*index=5*/s32[]{...) while((s32[]{:T(128)}, f32[8,8192]{1,0:T(8,128)S(1)}, ...), condition=%wide.region_24.25_spmd.clone, body=%wide.region_23.24_spmd.clone.sunk | while | flops 2162706 | bytes 4721599 | solution.py:71
  470.0 47.3 %all-reduce.18 = (f32[]{:T(128)}, f32[]{:T(128)}) all-reduce(f32[]{:T(128)} %get-tuple-element.1217, f32[]{:T(128)} %fusion.138), channel_id=1, replica_groups=mesh['rows'=8,'scales'=4] {'rows','scales'}, use_global_device_ids=true, to_apply=%region_22.23 | all-reduce | flops 2 | bytes 16 | tf_op jit(solution)/shard_map/psum | solution.py:128
  519.4 18.3 %all-gather.6.cloned.1.call-done = f32[32,8192]{1,0:T(8,128)} async-done(((f32[8,8192]{1,0:T(8,128)}), f32[32,8192]{1,0:T(8,128)}) %all-gather.6.cloned.1.call-update) | async-done | bytes 1048592 | tf_op jit(solution)/shard_map/all_gather | solution.py:134
  537.6 4.2 multiply_add_fusion.2
  548.6 5.5 all-to-all-start.4
  555.2 25.1 %all-to-all-done.4 = f32[32,8,1024]{2,0,1:T(8,128)S(1)} async-done(((f32[32,8,1024]{2,0,1:T(8,128)}), f32[32,8,1024]{2,0,1:T(8,128)S(1)}, u32[]{:S(2)}, u32[]{:S(2)}) %all-to-all-start.4) | async-done | bytes 1048608 | tf_op jit(solution)/shard_map/all_to_all | solution.py:146
  580.3 3.6 all-to-all-start.3
  585.4 24.4 %all-to-all-done.3 = f32[32,8,1024]{2,0,1:T(8,128)S(1)} async-done(((f32[32,8,1024]{2,0,1:T(8,128)}), f32[32,8,1024]{2,0,1:T(8,128)S(1)}, u32[]{:S(2)}, u32[]{:S(2)}) %all-to-all-start.3) | async-done | bytes 1048608 | tf_op jit(solution)/shard_map/all_to_all | solution.py:145
  610.2 30.1 %all_to_all.115 = f32[8,32,1024]{2,1,0:T(8,128)S(1)} all-to-all(f32[8,32,1024]{2,1,0:T(8,128)S(1)} %bitcast.71), channel_id=1, replica_groups=mesh['rows'=8,'scales'=4] {'rows'}, dimensions={0} | all-to-all | bytes 2097152 | tf_op jit(solution)/shard_map/all_to_all | solution.py:156
  641.4 24.8 %reduce-scatter.5.cloned.1.call-done = f32[8,8192]{1,0:T(8,128)} async-done(((f32[32,8192]{1,0:T(8,128)}), f32[8,8192]{1,0:T(8,128)}) %reduce-scatter.5.cloned.1.call-update) | async-done | bytes 262160 | tf_op jit(solution)/shard_map/reduce_scatter | solution.py:157
  (383 shorter events, 218.1 us)
Async XLA Ops:
  6.5 219.3 %all-gather.4.cloned.1.call-start = ((), (), s32[]{:S(2)}) async-start(), calls=%async_computation.8 | async-start | bytes 1310720 | tf_op jit(solution)/shard_map/all_gather | solution.py:134
  7.6 50.3 %collective-permute-start.2 = (f32[8,8192]{1,0:T(8,128)S(1)}, f32[8,8192]{1,0:T(8,128)S(1)}, u32[]{:S(2)}, u32[]{:S(2)}) collective-permute-start(f32[8,8192]{1,0:T(8,128)S(1)} %sub.46), channel_id=1, source_target_pairs={{0,1},{1,2},{2,3},{3,4},{4,5},{5,6},{6,7},{7,8},{8,9},{9,10},{10,1... | collective-permute-start | bytes 786440 | tf_op jit(solution)/shard_map/ppermute | solution.py:21
  10.0 47.9 %collective-permute-start.3 = (f32[8,8192]{1,0:T(8,128)S(1)}, f32[8,8192]{1,0:T(8,128)S(1)}, u32[]{:S(2)}, u32[]{:S(2)}) collective-permute-start(f32[8,8192]{1,0:T(8,128)S(1)} %sub.46), channel_id=1, source_target_pairs={{1,0},{2,1},{3,2},{4,3},{5,4},{6,5},{7,6},{8,7},{9,8},{10,9},{11,1... | collective-permute-start | bytes 786440 | tf_op jit(solution)/shard_map/ppermute | solution.py:23
  58.2 27.8 %copy-start = (f32[8,8192]{1,0:T(8,128)S(1)}, f32[8,8192]{1,0:T(8,128)}, u32[]{:S(2)}) copy-start(f32[8,8192]{1,0:T(8,128)} %param.29) | copy-start | bytes 786436
  86.1 10.6 %collective-permute-start.4 = (f32[8,8192]{1,0:T(8,128)S(1)}, f32[8,8192]{1,0:T(8,128)S(1)}, u32[]{:S(2)}, u32[]{:S(2)}) collective-permute-start(f32[8,8192]{1,0:T(8,128)S(1)} %mul.2942), channel_id=1, source_target_pairs={{0,1},{1,2},{2,3},{3,4},{4,5},{5,6},{6,7},{7,8},{8,9},{9,10},{10,1... | collective-permute-start | bytes 786440 | tf_op jit(solution)/shard_map/ppermute | solution.py:21
  88.4 8.4 %collective-permute-start.5 = (f32[8,8192]{1,0:T(8,128)S(1)}, f32[8,8192]{1,0:T(8,128)S(1)}, u32[]{:S(2)}, u32[]{:S(2)}) collective-permute-start(f32[8,8192]{1,0:T(8,128)S(1)} %mul.2942), channel_id=1, source_target_pairs={{1,0},{2,1},{3,2},{4,3},{5,4},{6,5},{7,6},{8,7},{9,8},{10,9},{11,1... | collective-permute-start | bytes 786440 | tf_op jit(solution)/shard_map/ppermute | solution.py:23
  89.7 4.4 collective-permute-start
  92.7 3.8 collective-permute-start.1
  97.0 29.6 %copy-start.5 = (f32[8,8192]{1,0:T(8,128)S(1)}, f32[8,8192]{1,0:T(8,128)}, u32[]{:S(2)}) copy-start(f32[8,8192]{1,0:T(8,128)} %param.28) | copy-start | bytes 786436
  127.3 5.6 collective-permute-start.6
  131.6 3.4 collective-permute-start.7
  135.3 72.4 %copy-start.1 = (f32[8,8192]{1,0:T(8,128)S(1)}, f32[8,8192]{1,0:T(8,128)}, u32[]{:S(2)}) copy-start(f32[8,8192]{1,0:T(8,128)} %param.27) | copy-start | bytes 786436
  230.0 1.2 copy-start.2
  236.8 31.7 %all-to-all-start.1 = ((f32[32,8,1024]{2,0,1:T(8,128)}), f32[32,8,1024]{2,0,1:T(8,128)S(1)}, u32[]{:S(2)}, u32[]{:S(2)}) async-start(f32[32,8,1024]{2,0,1:T(8,128)} %bitcast.50), calls=%async_computation.1 | async-start | bytes 2097152 | tf_op jit(solution)/shard_map/all_to_all | solution.py:146
  268.5 3.8 copy-start.6
  268.5 29.7 %all-to-all-start = ((f32[32,8,1024]{2,0,1:T(8,128)}), f32[32,8,1024]{2,0,1:T(8,128)S(1)}, u32[]{:S(2)}, u32[]{:S(2)}) async-start(f32[32,8,1024]{2,0,1:T(8,128)} %bitcast.68), calls=%async_computation | async-start | bytes 2097152 | tf_op jit(solution)/shard_map/all_to_all | solution.py:145
  272.3 82.3 %reduce-scatter.3.cloned.1.call-start = ((), (), s32[]{:S(2)}) async-start(), calls=%async_computation.9 | async-start | bytes 1310720 | tf_op jit(solution)/shard_map/reduce_scatter | solution.py:157
  329.8 207.8 %all-gather.6.cloned.1.call-start = ((), (), s32[]{:S(2)}) async-start(), calls=%async_computation.10 | async-start | bytes 1310720 | tf_op jit(solution)/shard_map/all_gather | solution.py:134
  355.6 2.9 collective-permute-start.8
  357.2 3.7 collective-permute-start.9
  389.0 8.2 %collective-permute-start.10 = (f32[8,8192]{1,0:T(8,128)S(1)}, f32[8,8192]{1,0:T(8,128)S(1)}, u32[]{:S(2)}, u32[]{:S(2)}) collective-permute-start(f32[8,8192]{1,0:T(8,128)S(1)} %mul.2961), channel_id=1, source_target_pairs={{0,1},{1,2},{2,3},{3,4},{4,5},{5,6},{6,7},{7,8},{8,9},{9,10},{10,1... | collective-permute-start | bytes 786440 | tf_op jit(solution)/shard_map/ppermute | solution.py:21
  395.7 3.4 collective-permute-start.11
  429.6 9.4 %collective-permute-start.12 = (f32[8,8192]{1,0:T(8,128)S(1)}, f32[8,8192]{1,0:T(8,128)S(1)}, u32[]{:S(2)}, u32[]{:S(2)}) collective-permute-start(f32[8,8192]{1,0:T(8,128)S(1)} %get-tuple-element.1218), channel_id=1, source_target_pairs={{0,1},{1,2},{2,3},{3,4},{4,5},{5,6},{6,7},{7,8},{8,9},{9,10},{10,1... | collective-permute-start | bytes 786440 | tf_op jit(solution)/shard_map/ppermute | solution.py:21
  437.7 3.4 collective-permute-start.13
  441.4 77.2 %copy-start.4 = (f32[8,8192]{1,0:T(8,128)S(1)}, f32[8,8192]{1,0:T(8,128)}, u32[]{:S(2)}) copy-start(f32[8,8192]{1,0:T(8,128)} %reduce-scatter.3.cloned.1.call-done) | copy-start | bytes 786436
  541.8 1.2 copy-start.3
  548.6 31.7 %all-to-all-start.4 = ((f32[32,8,1024]{2,0,1:T(8,128)}), f32[32,8,1024]{2,0,1:T(8,128)S(1)}, u32[]{:S(2)}, u32[]{:S(2)}) async-start(f32[32,8,1024]{2,0,1:T(8,128)} %bitcast.48), calls=%async_computation.5 | async-start | bytes 2097152 | tf_op jit(solution)/shard_map/all_to_all | solution.py:146
  580.3 29.6 %all-to-all-start.3 = ((f32[32,8,1024]{2,0,1:T(8,128)}), f32[32,8,1024]{2,0,1:T(8,128)S(1)}, u32[]{:S(2)}, u32[]{:S(2)}) async-start(f32[32,8,1024]{2,0,1:T(8,128)} %bitcast.49), calls=%async_computation.4 | async-start | bytes 2097152 | tf_op jit(solution)/shard_map/all_to_all | solution.py:145
  583.9 82.3 %reduce-scatter.5.cloned.1.call-start = ((), (), s32[]{:S(2)}) async-start(), calls=%async_computation.11 | async-start | bytes 1310720 | tf_op jit(solution)/shard_map/reduce_scatter | solution.py:157
Sparse Core Ops, SparseCore 0:
  208.6 17.2 all-gather.3
  329.9 24.6 reduce-scatter.2
  519.5 18.0 all-gather.5
  641.5 24.6 reduce-scatter.4
where the time goes:
time: 674 us; the launch traced here: 673 us
  blocking collectives  196 us (29%)
  waiting for transfers between devices  195 us (29%)
  other arithmetic  156 us (23%)
  starting transfers between devices  56.1 us (8%)
  local copies, waits for them, and re-layouts  49.5 us (7%)
  between operations  17.6 us (3%)
    psum x2, blocking collectives, body(): lax.psum((jnp.sum(descent * descent), jnp.sum(hessian_weight * blurred *...  89.8 us
    add x64, other arithmetic, forward_add_tap_row(): summed + tap_weights[:, column:column + 1] * shifted[:, column:column + c...  81 us
    all_to_all x2, blocking collectives, body(): lax.all_to_all(kept, 'rows', split_axis=0, concat_axis=1, tiled=True)  60.3 us
    all_to_all x2, waiting for transfers between devices, body(): lax.all_to_all(upper, 'rows', split_axis=1, concat_axis=0, tiled=True)  50.2 us
    reduce_scatter x2, waiting for transfers between devices, body(): lax.psum_scatter(contribution, 'scales', scatter_dimension=0, tiled=True)  49.5 us
    all_to_all x2, waiting for transfers between devices, body(): lax.all_to_all(lower, 'rows', split_axis=1, concat_axis=0, tiled=True)  48.3 us
    all_gather x1, blocking collectives, body(): tiles_in = lax.all_gather(psf_tiles, ('rows', 'scales'), axis=0, tiled=True)  45.4 us
    add x32, other arithmetic, adjoint_add_tap_row(): summed + tap_weights[:, column:column + 1] * shifted[:, offset_col:offset...  43.6 us
  transfers between devices with their start and end apart: 22, of which 13 were waited for; matrix products, arithmetic and copies ran while one was open for 1% of the time, Pallas kernels for 0%

commit v1 on v0

--- a/solution.py
+++ b/solution.py
@@ -153,7 +153,11 @@
             - jnp.clip(detail, -limit, limit)
             + jnp.where(scale_index == scale_count - 1, upper_cols, 0.0)
         )
-        contribution = lax.all_to_all(kept, "rows", split_axis=0, concat_axis=1, tiled=True)
+        y1 = jax.lax.psum(1, "rows")
+        outer = jnp.split(kept, y1, 0)
+        ready = jnp.stack(outer, 0)
+        arr_out = jax.lax.all_to_all(ready, "rows", 0, 0)
+        contribution = jnp.concatenate(arr_out, 1)
         current = lax.psum_scatter(contribution, "scales", scatter_dimension=0, tiled=True)
     return current
 

time: 674 us -> 674 us (level)
  no operation moved by 1% of the time
where the time goes in v1:
time: 674 us; the launch traced here: 673 us
  blocking collectives  196 us (29%)
  waiting for transfers between devices  195 us (29%)
  other arithmetic  156 us (23%)
  starting transfers between devices  56.1 us (8%)
  local copies, waits for them, and re-layouts  49.7 us (7%)
  between operations  17.7 us (3%)
    psum x2, blocking collectives, body(): lax.psum((jnp.sum(descent * descent), jnp.sum(hessian_weight * blurred *...  89.8 us
    add x64, other arithmetic, forward_add_tap_row(): summed + tap_weights[:, column:column + 1] * shifted[:, column:column + c...  81 us
    all_to_all x2, blocking collectives, body(): arr_out = jax.lax.all_to_all(ready, 'rows', 0, 0)  60.3 us
    all_to_all x2, waiting for transfers between devices, body(): lax.all_to_all(upper, 'rows', split_axis=1, concat_axis=0, tiled=True)  50.2 us
    reduce_scatter x2, waiting for transfers between devices, body(): lax.psum_scatter(contribution, 'scales', scatter_dimension=0, tiled=True)  49.5 us
    all_to_all x2, waiting for transfers between devices, body(): lax.all_to_all(lower, 'rows', split_axis=1, concat_axis=0, tiled=True)  48.3 us
    all_gather x1, blocking collectives, body(): tiles_in = lax.all_gather(psf_tiles, ('rows', 'scales'), axis=0, tiled=True)  45.4 us
    add x32, other arithmetic, adjoint_add_tap_row(): summed + tap_weights[:, column:column + 1] * shifted[:, offset_col:offset...  43.6 us
  transfers between devices with their start and end apart: 22, of which 13 were waited for; matrix products, arithmetic and copies ran while one was open for 1% of the time, Pallas kernels for 0%

profile of v1, /device:TPU:0, one launch (start us, length us, event | category | flops | bytes accessed | tf_op | source)
XLA Modules:
  0.0 673.3 jit_solution(17113526929602176010)
XLA Ops:
  7.6 2.4 collective-permute-start.2
  12.2 45.4 %all-gather = f32[32,1,256]{2,1,0:T(1,128)S(1)} all-gather(f32[1,1,256]{2,1,0:T(1,128)} %bitcast.139), channel_id=1, replica_groups=mesh['rows'=8,'scales'=4] {'rows','scales'}, dimensions={0}, use_global_device_ids=true | all-gather | bytes 33792 | tf_op jit(solution)/shard_map/all_gather | solution.py:105
  58.2 27.8 %while.146 = (s32[]{:T(128)}, f32[8,8192]{1,0:T(8,128)S(1)}, f32[8,16,16]{2,0,1:T(8,128)S(1)}, f32[24,8208]{1,0:T(8,128)S(1)}, s32[]{:T(128)}, /*index=5*/s32[]{...) while((s32[]{:T(128)}, f32[8,8192]{1,0:T(8,128)S(1)}, ...), condition=%wide.region_2.3_spmd.clone, body=%wide.region_1.2_spmd.clone.sunk | while | flops 2162706 | bytes 4721599 | solution.py:71
  89.7 3.0 collective-permute-start
  94.0 2.5 collective-permute-done.1
  97.0 29.6 %while.147 = (s32[]{:T(128)}, f32[8,8192]{1,0:T(8,128)S(1)}, f32[24,16,16]{2,0,1:T(8,128)S(1)}, f32[24,8208]{1,0:T(8,128)S(1)}, s32[]{:T(128)}, /*index=5*/s32[]...) while((s32[]{:T(128)}, f32[8,8192]{1,0:T(8,128)S(1)}, ...), condition=%wide.region_4.5_spmd.clone, body=%wide.region_3.4_spmd.clone.sunk | while | flops 2162713 | bytes 4721729 | solution.py:93
  127.3 4.3 collective-permute-start.6
  135.3 27.8 %while.148 = (s32[]{:T(128)}, f32[8,8192]{1,0:T(8,128)S(1)}, f32[8,16,16]{2,0,1:T(8,128)S(1)}, f32[24,8208]{1,0:T(8,128)S(1)}, s32[]{:T(128)}, /*index=5*/s32[]{...) while((s32[]{:T(128)}, f32[8,8192]{1,0:T(8,128)S(1)}, ...), condition=%wide.region_8.9_spmd.clone, body=%wide.region_7.8_spmd.clone.sunk | while | flops 2162706 | bytes 4721599 | solution.py:71
  163.9 42.4 %all-reduce.19 = (f32[]{:T(128)}, f32[]{:T(128)}) all-reduce(f32[]{:T(128)} %get-tuple-element.1221, f32[]{:T(128)} %fusion.137), channel_id=1, replica_groups=mesh['rows'=8,'scales'=4] {'rows','scales'}, use_global_device_ids=true, to_apply=%region_6.7 | all-reduce | flops 2 | bytes 16 | tf_op jit(solution)/shard_map/psum | solution.py:128
  208.5 17.4 %all-gather.4.cloned.1.call-done = f32[32,8192]{1,0:T(8,128)} async-done(((f32[8,8192]{1,0:T(8,128)}), f32[32,8192]{1,0:T(8,128)}) %all-gather.4.cloned.1.call-update) | async-done | bytes 1048592 | tf_op jit(solution)/shard_map/all_gather | solution.py:134
  225.8 4.2 multiply_add_fusion.5
  236.8 5.5 all-to-all-start.1
  243.4 25.1 %all-to-all-done.1 = f32[32,8,1024]{2,0,1:T(8,128)S(1)} async-done(((f32[32,8,1024]{2,0,1:T(8,128)}), f32[32,8,1024]{2,0,1:T(8,128)S(1)}, u32[]{:S(2)}, u32[]{:S(2)}) %all-to-all-start.1) | async-done | bytes 1048608 | tf_op jit(solution)/shard_map/all_to_all | solution.py:146
  268.5 3.8 all-to-all-start
  274.4 23.8 %all-to-all-done = f32[32,8,1024]{2,0,1:T(8,128)S(1)} async-done(((f32[32,8,1024]{2,0,1:T(8,128)}), f32[32,8,1024]{2,0,1:T(8,128)S(1)}, u32[]{:S(2)}, u32[]{:S(2)}) %all-to-all-start) | async-done | bytes 1048608 | tf_op jit(solution)/shard_map/all_to_all | solution.py:145
  298.7 30.1 %all_to_all.86 = f32[8,32,1024]{2,1,0:T(8,128)S(1)} all-to-all(f32[8,32,1024]{2,1,0:T(8,128)S(1)} %fusion.147), channel_id=1, replica_groups=mesh['rows'=8,'scales'=4] {'rows'}, dimensions={0} | all-to-all | bytes 2097152 | tf_op jit(solution)/shard_map/all_to_all | solution.py:159
  330.0 24.7 %reduce-scatter.3.cloned.1.call-done = f32[8,8192]{1,0:T(8,128)} async-done(((f32[32,8192]{1,0:T(8,128)}), f32[8,8192]{1,0:T(8,128)}) %reduce-scatter.3.cloned.1.call-update) | async-done | bytes 262160 | tf_op jit(solution)/shard_map/reduce_scatter | solution.py:161
  358.6 2.4 collective-permute-done.9
  361.3 27.8 %while.149 = (s32[]{:T(128)}, f32[8,8192]{1,0:T(8,128)S(1)}, f32[8,16,16]{2,0,1:T(8,128)S(1)}, f32[24,8208]{1,0:T(8,128)S(1)}, s32[]{:T(128)}, /*index=5*/s32[]{...) while((s32[]{:T(128)}, f32[8,8192]{1,0:T(8,128)S(1)}, ...), condition=%wide.region_18.19_spmd.clone, body=%wide.region_17.18_spmd.clone.sunk | while | flops 2162706 | bytes 4721599 | solution.py:71
  389.2 6.7 collective-permute-start.10
  399.8 29.6 %while.150 = (s32[]{:T(128)}, f32[8,8192]{1,0:T(8,128)S(1)}, f32[24,16,16]{2,0,1:T(8,128)S(1)}, f32[24,8208]{1,0:T(8,128)S(1)}, s32[]{:T(128)}, /*index=5*/s32[]...) while((s32[]{:T(128)}, f32[8,8192]{1,0:T(8,128)S(1)}, ...), condition=%wide.region_20.21_spmd.clone, body=%wide.region_19.20_spmd.clone.sunk | while | flops 2162713 | bytes 4721729 | solution.py:93
  430.0 8.0 %collective-permute-start.12 = (f32[8,8192]{1,0:T(8,128)S(1)}, f32[8,8192]{1,0:T(8,128)S(1)}, u32[]{:S(2)}, u32[]{:S(2)}) collective-permute-start(f32[8,8192]{1,0:T(8,128)S(1)} %get-tuple-element.1218), channel_id=1, source_target_pairs={{0,1},{1,2},{2,3},{3,4},{4,5},{5,6},{6,7},{7,8},{8,9},{9,10},{10,1... | collective-permute-start | bytes 786440 | tf_op jit(solution)/shard_map/ppermute | solution.py:21
  441.8 27.8 %while.151 = (s32[]{:T(128)}, f32[8,8192]{1,0:T(8,128)S(1)}, f32[8,16,16]{2,0,1:T(8,128)S(1)}, f32[24,8208]{1,0:T(8,128)S(1)}, s32[]{:T(128)}, /*index=5*/s32[]{...) while((s32[]{:T(128)}, f32[8,8192]{1,0:T(8,128)S(1)}, ...), condition=%wide.region_24.25_spmd.clone, body=%wide.region_23.24_spmd.clone.sunk | while | flops 2162706 | bytes 4721599 | solution.py:71
  470.3 47.3 %all-reduce.18 = (f32[]{:T(128)}, f32[]{:T(128)}) all-reduce(f32[]{:T(128)} %get-tuple-element.1217, f32[]{:T(128)} %fusion.138), channel_id=1, replica_groups=mesh['rows'=8,'scales'=4] {'rows','scales'}, use_global_device_ids=true, to_apply=%region_22.23 | all-reduce | flops 2 | bytes 16 | tf_op jit(solution)/shard_map/psum | solution.py:128
  519.7 18.3 %all-gather.6.cloned.1.call-done = f32[32,8192]{1,0:T(8,128)} async-done(((f32[8,8192]{1,0:T(8,128)}), f32[32,8192]{1,0:T(8,128)}) %all-gather.6.cloned.1.call-update) | async-done | bytes 1048592 | tf_op jit(solution)/shard_map/all_gather | solution.py:134
  538.0 4.2 multiply_add_fusion.2
  549.0 5.5 all-to-all-start.4
  555.5 25.1 %all-to-all-done.4 = f32[32,8,1024]{2,0,1:T(8,128)S(1)} async-done(((f32[32,8,1024]{2,0,1:T(8,128)}), f32[32,8,1024]{2,0,1:T(8,128)S(1)}, u32[]{:S(2)}, u32[]{:S(2)}) %all-to-all-start.4) | async-done | bytes 1048608 | tf_op jit(solution)/shard_map/all_to_all | solution.py:146
  580.6 3.6 all-to-all-start.3
  585.8 24.4 %all-to-all-done.3 = f32[32,8,1024]{2,0,1:T(8,128)S(1)} async-done(((f32[32,8,1024]{2,0,1:T(8,128)}), f32[32,8,1024]{2,0,1:T(8,128)S(1)}, u32[]{:S(2)}, u32[]{:S(2)}) %all-to-all-start.3) | async-done | bytes 1048608 | tf_op jit(solution)/shard_map/all_to_all | solution.py:145
  610.7 30.1 %all_to_all.87 = f32[8,32,1024]{2,1,0:T(8,128)S(1)} all-to-all(f32[8,32,1024]{2,1,0:T(8,128)S(1)} %fusion.139), channel_id=1, replica_groups=mesh['rows'=8,'scales'=4] {'rows'}, dimensions={0} | all-to-all | bytes 2097152 | tf_op jit(solution)/shard_map/all_to_all | solution.py:159
  641.9 24.8 %reduce-scatter.5.cloned.1.call-done = f32[8,8192]{1,0:T(8,128)} async-done(((f32[32,8192]{1,0:T(8,128)}), f32[8,8192]{1,0:T(8,128)}) %reduce-scatter.5.cloned.1.call-update) | async-done | bytes 262160 | tf_op jit(solution)/shard_map/reduce_scatter | solution.py:161
  (399 shorter events, 218.5 us)
Async XLA Ops:
  6.5 219.3 %all-gather.4.cloned.1.call-start = ((), (), s32[]{:S(2)}) async-start(), calls=%async_computation.8 | async-start | bytes 1310720 | tf_op jit(solution)/shard_map/all_gather | solution.py:134
  7.6 50.3 %collective-permute-start.2 = (f32[8,8192]{1,0:T(8,128)S(1)}, f32[8,8192]{1,0:T(8,128)S(1)}, u32[]{:S(2)}, u32[]{:S(2)}) collective-permute-start(f32[8,8192]{1,0:T(8,128)S(1)} %sub.46), channel_id=1, source_target_pairs={{0,1},{1,2},{2,3},{3,4},{4,5},{5,6},{6,7},{7,8},{8,9},{9,10},{10,1... | collective-permute-start | bytes 786440 | tf_op jit(solution)/shard_map/ppermute | solution.py:21
  10.0 47.9 %collective-permute-start.3 = (f32[8,8192]{1,0:T(8,128)S(1)}, f32[8,8192]{1,0:T(8,128)S(1)}, u32[]{:S(2)}, u32[]{:S(2)}) collective-permute-start(f32[8,8192]{1,0:T(8,128)S(1)} %sub.46), channel_id=1, source_target_pairs={{1,0},{2,1},{3,2},{4,3},{5,4},{6,5},{7,6},{8,7},{9,8},{10,9},{11,1... | collective-permute-start | bytes 786440 | tf_op jit(solution)/shard_map/ppermute | solution.py:23
  58.2 27.8 %copy-start = (f32[8,8192]{1,0:T(8,128)S(1)}, f32[8,8192]{1,0:T(8,128)}, u32[]{:S(2)}) copy-start(f32[8,8192]{1,0:T(8,128)} %param.29) | copy-start | bytes 786436
  86.1 10.6 %collective-permute-start.4 = (f32[8,8192]{1,0:T(8,128)S(1)}, f32[8,8192]{1,0:T(8,128)S(1)}, u32[]{:S(2)}, u32[]{:S(2)}) collective-permute-start(f32[8,8192]{1,0:T(8,128)S(1)} %mul.2942), channel_id=1, source_target_pairs={{0,1},{1,2},{2,3},{3,4},{4,5},{5,6},{6,7},{7,8},{8,9},{9,10},{10,1... | collective-permute-start | bytes 786440 | tf_op jit(solution)/shard_map/ppermute | solution.py:21
  88.4 8.4 %collective-permute-start.5 = (f32[8,8192]{1,0:T(8,128)S(1)}, f32[8,8192]{1,0:T(8,128)S(1)}, u32[]{:S(2)}, u32[]{:S(2)}) collective-permute-start(f32[8,8192]{1,0:T(8,128)S(1)} %mul.2942), channel_id=1, source_target_pairs={{1,0},{2,1},{3,2},{4,3},{5,4},{6,5},{7,6},{8,7},{9,8},{10,9},{11,1... | collective-permute-start | bytes 786440 | tf_op jit(solution)/shard_map/ppermute | solution.py:23
  89.7 4.4 collective-permute-start
  92.7 3.8 collective-permute-start.1
  97.0 29.6 %copy-start.5 = (f32[8,8192]{1,0:T(8,128)S(1)}, f32[8,8192]{1,0:T(8,128)}, u32[]{:S(2)}) copy-start(f32[8,8192]{1,0:T(8,128)} %param.28) | copy-start | bytes 786436
  127.3 5.6 collective-permute-start.6
  131.6 3.4 collective-permute-start.7
  135.3 72.4 %copy-start.1 = (f32[8,8192]{1,0:T(8,128)S(1)}, f32[8,8192]{1,0:T(8,128)}, u32[]{:S(2)}) copy-start(f32[8,8192]{1,0:T(8,128)} %param.27) | copy-start | bytes 786436
  230.0 1.2 copy-start.2
  236.8 31.7 %all-to-all-start.1 = ((f32[32,8,1024]{2,0,1:T(8,128)}), f32[32,8,1024]{2,0,1:T(8,128)S(1)}, u32[]{:S(2)}, u32[]{:S(2)}) async-start(f32[32,8,1024]{2,0,1:T(8,128)} %bitcast.112), calls=%async_computation.1 | async-start | bytes 2097152 | tf_op jit(solution)/shard_map/all_to_all | solution.py:146
  268.5 3.8 copy-start.6
  268.5 29.7 %all-to-all-start = ((f32[32,8,1024]{2,0,1:T(8,128)}), f32[32,8,1024]{2,0,1:T(8,128)S(1)}, u32[]{:S(2)}, u32[]{:S(2)}) async-start(f32[32,8,1024]{2,0,1:T(8,128)} %bitcast.130), calls=%async_computation | async-start | bytes 2097152 | tf_op jit(solution)/shard_map/all_to_all | solution.py:145
  272.3 82.5 %reduce-scatter.3.cloned.1.call-start = ((), (), s32[]{:S(2)}) async-start(), calls=%async_computation.9 | async-start | bytes 1310720 | tf_op jit(solution)/shard_map/reduce_scatter | solution.py:161
  330.0 208.0 %all-gather.6.cloned.1.call-start = ((), (), s32[]{:S(2)}) async-start(), calls=%async_computation.10 | async-start | bytes 1310720 | tf_op jit(solution)/shard_map/all_gather | solution.py:134
  355.7 2.9 collective-permute-start.8
  357.3 3.7 collective-permute-start.9
  389.2 8.2 %collective-permute-start.10 = (f32[8,8192]{1,0:T(8,128)S(1)}, f32[8,8192]{1,0:T(8,128)S(1)}, u32[]{:S(2)}, u32[]{:S(2)}) collective-permute-start(f32[8,8192]{1,0:T(8,128)S(1)} %mul.2961), channel_id=1, source_target_pairs={{0,1},{1,2},{2,3},{3,4},{4,5},{5,6},{6,7},{7,8},{8,9},{9,10},{10,1... | collective-permute-start | bytes 786440 | tf_op jit(solution)/shard_map/ppermute | solution.py:21
  395.8 3.6 collective-permute-start.11
  430.0 9.4 %collective-permute-start.12 = (f32[8,8192]{1,0:T(8,128)S(1)}, f32[8,8192]{1,0:T(8,128)S(1)}, u32[]{:S(2)}, u32[]{:S(2)}) collective-permute-start(f32[8,8192]{1,0:T(8,128)S(1)} %get-tuple-element.1218), channel_id=1, source_target_pairs={{0,1},{1,2},{2,3},{3,4},{4,5},{5,6},{6,7},{7,8},{8,9},{9,10},{10,1... | collective-permute-start | bytes 786440 | tf_op jit(solution)/shard_map/ppermute | solution.py:21
  438.1 3.4 collective-permute-start.13
  441.8 77.2 %copy-start.4 = (f32[8,8192]{1,0:T(8,128)S(1)}, f32[8,8192]{1,0:T(8,128)}, u32[]{:S(2)}) copy-start(f32[8,8192]{1,0:T(8,128)} %reduce-scatter.3.cloned.1.call-done) | copy-start | bytes 786436
  542.2 1.2 copy-start.3
  549.0 31.7 %all-to-all-start.4 = ((f32[32,8,1024]{2,0,1:T(8,128)}), f32[32,8,1024]{2,0,1:T(8,128)S(1)}, u32[]{:S(2)}, u32[]{:S(2)}) async-start(f32[32,8,1024]{2,0,1:T(8,128)} %bitcast.110), calls=%async_computation.5 | async-start | bytes 2097152 | tf_op jit(solution)/shard_map/all_to_all | solution.py:146
  580.6 29.6 %all-to-all-start.3 = ((f32[32,8,1024]{2,0,1:T(8,128)}), f32[32,8,1024]{2,0,1:T(8,128)S(1)}, u32[]{:S(2)}, u32[]{:S(2)}) async-start(f32[32,8,1024]{2,0,1:T(8,128)} %bitcast.111), calls=%async_computation.4 | async-start | bytes 2097152 | tf_op jit(solution)/shard_map/all_to_all | solution.py:145
  584.3 82.5 %reduce-scatter.5.cloned.1.call-start = ((), (), s32[]{:S(2)}) async-start(), calls=%async_computation.11 | async-start | bytes 1310720 | tf_op jit(solution)/shard_map/reduce_scatter | solution.py:161
Sparse Core Ops, SparseCore 0:
  208.6 17.2 all-gather.3
  330.1 24.6 reduce-scatter.2
  519.9 18.0 all-gather.5
  642.1 24.6 reduce-scatter.4
